TPU v7x, 32 devices: a whole 2x2x4 slice. The times are simulated.
32 devices in a mesh: mem: 8 (over z, y), band: 4 (over x, core).
Axes of the slice: x: 2, y: 2, z: 4, core: 2. Of those that a mesh axis runs over, the one named last changes fastest.
Arguments:
- ensemble: float32 [256, 256, 256], P('mem', 'band'), may hold values from -8 to 8
- column_operator: float32 [128, 128], replicated, may hold values from -0.5 to 0.5
- patch_order: int32 [4, 64], P('band'), may hold values from 0 to 63, as said below
- obs_index: int32 [4, 64, 512], P('band'), may hold values from 0 to 255
- obs_count: int32 [4, 64], P('band', 'mem'), may hold values from 1 to 512
- obs_values: float32 [4, 64, 512], P('band', 'mem'), may hold values from -8 to 8
- obs_precision: float32 [4, 64, 512], P('band', 'mem'), may hold values from 2 to 50
Outputs:
- analysis: float32 [256, 256, 256], P('mem', 'band')
- transform: float32 [4, 64, 256, 256], P('band', 'mem')
Inputs may be any that keep to these rules, and one draw needn't show every extreme that they name: `patch_order`: each row is a permutation of 0 to 63.
All inputs are finite; a program needn't handle non-finite values.
Results may differ from a plain program's by a relative error of at most 0.0003.
Values sent between devices are 32-bit elements; how exact they have to be, the bound alone decides.
A program may use at most 64 MiB of HBM per device.

v0:
```python
import math
import jax
import jax.numpy as jnp
from jax import lax
from jax.sharding import PartitionSpec as P

ITERS = 12


def batched(left, right):
    return jnp.einsum("pij,pjk->pik", left, right, precision=lax.Precision.HIGHEST)


def map_columns(states, column_operator):
    rows, patches, cells = states.shape
    levels = column_operator.shape[0]
    flat_rows = states.reshape(rows * patches * (cells // levels), levels)
    mapped = jnp.dot(flat_rows, column_operator, precision=lax.Precision.HIGHEST)
    return mapped.reshape(rows, patches, -1)


def select_slots(channel_values, index):
    width = channel_values.shape[2]
    places = jnp.arange(width, dtype=jnp.int32)
    picker = (index[:, None, :] == places[None, :, None]).astype(jnp.float32)
    return jnp.einsum("kpc,pco->kpo", channel_values, picker, precision=lax.Precision.HIGHEST)


def local(ensemble, column_operator, patch_order, obs_index, obs_count, obs_values, obs_precision):
    highest = lax.Precision.HIGHEST
    members_dev, band_patches, cells = ensemble.shape
    slots = obs_index.shape[2]
    n_mem = lax.axis_size("mem")
    worker = lax.axis_index("mem")
    per_worker = band_patches // n_mem
    order = patch_order[0]
    positions = jnp.arange(band_patches, dtype=jnp.int32)
    permuter = (order[None, :] == positions[:, None]).astype(jnp.float32)
    listed = jnp.einsum("kqc,qj->kjc", ensemble, permuter, precision=highest)
    my_index = lax.dynamic_slice_in_dim(obs_index[0], worker * per_worker, per_worker, 0)
    state_in = lax.all_to_all(listed, "mem", split_axis=1, concat_axis=0, tiled=True)
    obs_block = select_slots(map_columns(state_in, column_operator), my_index)
    count = obs_count[0]
    values = obs_values[0]
    precision = obs_precision[0]
    members = obs_block.shape[0]
    live = (jnp.arange(slots, dtype=jnp.int32)[None, :] < count[:, None]).astype(jnp.float32)
    obs_weight = precision * live
    obs_mean = jnp.mean(obs_block, axis=0)
    obs_pert = obs_block - obs_mean
    innov = (values - obs_mean) * obs_weight
    gram = jnp.einsum("kpo,jpo->pkj", obs_pert * obs_weight, obs_pert, precision=highest)
    identity = jnp.eye(members, dtype=jnp.float32)
    system = gram + (members - 1.0) * identity
    trace_value = jnp.trace(system, axis1=1, axis2=2)
    level = system / trace_value[:, None, None]

    def sweep(step, carry):
        ymat, zmat = carry
        turn = 1.5 * identity - 0.5 * batched(zmat, ymat)
        return (batched(ymat, turn), batched(turn, zmat))

    ymat, zmat = lax.fori_loop(0, ITERS, sweep, (level, jnp.broadcast_to(identity, level.shape)))
    root = zmat / jnp.sqrt(trace_value)[:, None, None]
    spread = math.sqrt(members - 1.0) * root
    projected = jnp.einsum("kpo,po->pk", obs_pert, innov, precision=highest)
    inner = jnp.einsum("pij,pj->pi", root, projected, precision=highest)
    mean_weight = jnp.einsum("pij,pj->pi", root, inner, precision=highest)
    coef = spread + mean_weight[:, :, None]
    state_mean = jnp.mean(state_in, axis=0)
    state_pert = state_in - state_mean
    updated = state_mean + jnp.einsum("pjk,jpc->kpc", coef, state_pert, precision=highest)
    returned = lax.all_to_all(updated, "mem", split_axis=0, concat_axis=1, tiled=True)
    restored = jnp.einsum("kjc,qj->kqc", returned, permuter, precision=highest)
    return (restored, spread[None])


def solution(mesh):
    placed = (
        P("mem", "band", None),
        P(),
        P("band", None),
        P("band", None, None),
        P("band", "mem"),
        P("band", "mem", None),
        P("band", "mem", None),
    )
    return jax.shard_map(
        local,
        mesh=mesh,
        in_specs=placed,
        out_specs=(P("mem", "band", None), P("band", "mem", None, None)),
        check_vma=False,
    )
```

profile of v0, /device:TPU:0, one launch (start us, length us, event | category | flops | bytes accessed | tf_op | source)
XLA Modules:
  0.0 328.3 jit_solution(8018955491535311315)
XLA Ops:
  6.7 7.4 %all-to-all-start = ((f32[32,64,256]{2,0,1:T(8,128)}), f32[32,64,256]{2,0,1:T(8,128)}, u32[]{:S(2)}, u32[]{:S(2)}) async-start(f32[32,64,256]{2,0,1:T(8,128)} %copy.41), calls=%async_computation | async-start | bytes 4194304 | tf_op jit(solution)/shard_map/all_to_all | solution.py:41
  15.0 47.5 %all-to-all-done = f32[32,64,256]{2,0,1:T(8,128)} async-done(((f32[32,64,256]{2,0,1:T(8,128)}), f32[32,64,256]{2,0,1:T(8,128)}, u32[]{:S(2)}, u32[]{:S(2)}) %all-to-all-start) | async-done | bytes 2097184 | tf_op jit(solution)/shard_map/all_to_all | solution.py:41
  62.5 4.1 %copy.43 = f32[8,32,8,256]{3,2,1,0:T(8,128)} copy(f32[8,32,8,256]{3,1,2,0:T(8,128)} %bitcast.7) | data formatting | bytes 4194304 | tf_op jit(solution)/shard_map/all_to_all | solution.py:41
  81.1 4.3 %bitcast_reduce_fusion = (f32[8,512]{1,0:T(8,128)S(1)}, f32[8,512,256]{1,2,0:T(8,128)S(1)}) fusion(f32[256,8,256]{2,1,0:T(8,128)} %reshape.72, s32[8,512]{1,0:T(8,128)S(1)} %dynamic-slice_bitcast_fusion), kind=kOutput, calls=%fused_computation.16 | convolution fusion | flops 3223318528 | bytes 6324224 | tf_op jit(solution)/shard_map/kpc,pco->kpo/dot_general | solution.py:26
  85.5 3.7 %fusion.15 = f32[8,1,256]{2,1,0:T(1,128)S(1)} fusion(f32[8,512,256]{1,2,0:T(8,128)S(1)} %get-tuple-element.54, f32[8,512]{1,0:T(8,128)S(1)} %get-tuple-element.52, f32[8,512,1]{1,0,2:T(8,128)S(1)} %get-tuple-element.51), kind=kOutput, calls=%fused_computation.19 | convolution fusion | flops 13631488 | bytes 4235264 | tf_op jit(solution)/shard_map/kpo,po->pk/dot_general | solution.py:66
  89.2 4.7 %select_reduce_fusion = (f32[8]{0:T(128)S(1)}, f32[8,256,256]{2,1,0:T(8,128)S(1)}) fusion(f32[256,256]{1,0:T(8,128)S(1)} %fusion.38, pred[256,256]{1,0:T(8,128)(4,1)S(1)} %iota_compare_fusion.3, f32[8,512,256]{1,2,0:T(8,128)S(1)} %get-tuple-element.54, f32[8,512]{1,0:T(8,128)S(1)} %get-tuple-element.52, f32[8,512]{1,0:T(8,128)S(1)} %select_bitcast_fusion), kind=kOutput, calls=%fused_computation.30 | convolution fusion | flops 3225944064 | bytes 6651936 | tf_op jit(solution)/shard_map/kpo,jpo->pkj/dot_general | solution.py:52
  100.0 157.3 %while.13 = (s32[]{:T(128)}, f32[8,256,256]{1,2,0:T(8,128)}, f32[8,256,256]{2,1,0:T(8,128)}, s32[]{:T(128)}) while((s32[]{:T(128)}, f32[8,256,256]{1,2,0:T(8,128)}, f32[8,256,256]{2,1,0:T(8,128)}, s32[]{:T(128)}) %tuple.32), condition=%wide.region_4.5_spmd.clone, body=%wide.region_3.4_spmd.clone.sunk | while | flops 4834066432 | bytes 36438096 | solution.py:63
  104.7 4.9 %fusion.75 = f32[8,256,256]{1,2,0:T(8,128)} fusion(f32[8,256,256]{1,2,0:T(8,128)S(1)} %copy.103, f32[8,256,256]{2,1,0:T(8,128)S(1)} %fusion.73, f32[256,256]{1,0:T(8,128)S(1)} %fusion.74), kind=kOutput, calls=%fused_computation.4.clone.1 | convolution fusion | flops 1611661312 | bytes 6553600 | tf_op jit(solution)/shard_map/while/body/eval_jaxpr/pij,pjk->pik/dot_general | solution.py:11
  117.8 4.9 %fusion.75 = f32[8,256,256]{1,2,0:T(8,128)} fusion(f32[8,256,256]{1,2,0:T(8,128)S(1)} %copy.103, f32[8,256,256]{2,1,0:T(8,128)S(1)} %fusion.73, f32[256,256]{1,0:T(8,128)S(1)} %fusion.74), kind=kOutput, calls=%fused_computation.4.clone.1 | convolution fusion | flops 1611661312 | bytes 6553600 | tf_op jit(solution)/shard_map/while/body/eval_jaxpr/pij,pjk->pik/dot_general | solution.py:11
  130.9 4.9 %fusion.75 = f32[8,256,256]{1,2,0:T(8,128)} fusion(f32[8,256,256]{1,2,0:T(8,128)S(1)} %copy.103, f32[8,256,256]{2,1,0:T(8,128)S(1)} %fusion.73, f32[256,256]{1,0:T(8,128)S(1)} %fusion.74), kind=kOutput, calls=%fused_computation.4.clone.1 | convolution fusion | flops 1611661312 | bytes 6553600 | tf_op jit(solution)/shard_map/while/body/eval_jaxpr/pij,pjk->pik/dot_general | solution.py:11
  144.0 4.9 %fusion.75 = f32[8,256,256]{1,2,0:T(8,128)} fusion(f32[8,256,256]{1,2,0:T(8,128)S(1)} %copy.103, f32[8,256,256]{2,1,0:T(8,128)S(1)} %fusion.73, f32[256,256]{1,0:T(8,128)S(1)} %fusion.74), kind=kOutput, calls=%fused_computation.4.clone.1 | convolution fusion | flops 1611661312 | bytes 6553600 | tf_op jit(solution)/shard_map/while/body/eval_jaxpr/pij,pjk->pik/dot_general | solution.py:11
  157.1 4.9 %fusion.75 = f32[8,256,256]{1,2,0:T(8,128)} fusion(f32[8,256,256]{1,2,0:T(8,128)S(1)} %copy.103, f32[8,256,256]{2,1,0:T(8,128)S(1)} %fusion.73, f32[256,256]{1,0:T(8,128)S(1)} %fusion.74), kind=kOutput, calls=%fused_computation.4.clone.1 | convolution fusion | flops 1611661312 | bytes 6553600 | tf_op jit(solution)/shard_map/while/body/eval_jaxpr/pij,pjk->pik/dot_general | solution.py:11
  170.2 4.9 %fusion.75 = f32[8,256,256]{1,2,0:T(8,128)} fusion(f32[8,256,256]{1,2,0:T(8,128)S(1)} %copy.103, f32[8,256,256]{2,1,0:T(8,128)S(1)} %fusion.73, f32[256,256]{1,0:T(8,128)S(1)} %fusion.74), kind=kOutput, calls=%fused_computation.4.clone.1 | convolution fusion | flops 1611661312 | bytes 6553600 | tf_op jit(solution)/shard_map/while/body/eval_jaxpr/pij,pjk->pik/dot_general | solution.py:11
  183.3 4.9 %fusion.75 = f32[8,256,256]{1,2,0:T(8,128)} fusion(f32[8,256,256]{1,2,0:T(8,128)S(1)} %copy.103, f32[8,256,256]{2,1,0:T(8,128)S(1)} %fusion.73, f32[256,256]{1,0:T(8,128)S(1)} %fusion.74), kind=kOutput, calls=%fused_computation.4.clone.1 | convolution fusion | flops 1611661312 | bytes 6553600 | tf_op jit(solution)/shard_map/while/body/eval_jaxpr/pij,pjk->pik/dot_general | solution.py:11
  196.4 4.9 %fusion.75 = f32[8,256,256]{1,2,0:T(8,128)} fusion(f32[8,256,256]{1,2,0:T(8,128)S(1)} %copy.103, f32[8,256,256]{2,1,0:T(8,128)S(1)} %fusion.73, f32[256,256]{1,0:T(8,128)S(1)} %fusion.74), kind=kOutput, calls=%fused_computation.4.clone.1 | convolution fusion | flops 1611661312 | bytes 6553600 | tf_op jit(solution)/shard_map/while/body/eval_jaxpr/pij,pjk->pik/dot_general | solution.py:11
  209.5 4.9 %fusion.75 = f32[8,256,256]{1,2,0:T(8,128)} fusion(f32[8,256,256]{1,2,0:T(8,128)S(1)} %copy.103, f32[8,256,256]{2,1,0:T(8,128)S(1)} %fusion.73, f32[256,256]{1,0:T(8,128)S(1)} %fusion.74), kind=kOutput, calls=%fused_computation.4.clone.1 | convolution fusion | flops 1611661312 | bytes 6553600 | tf_op jit(solution)/shard_map/while/body/eval_jaxpr/pij,pjk->pik/dot_general | solution.py:11
  222.7 4.9 %fusion.75 = f32[8,256,256]{1,2,0:T(8,128)} fusion(f32[8,256,256]{1,2,0:T(8,128)S(1)} %copy.103, f32[8,256,256]{2,1,0:T(8,128)S(1)} %fusion.73, f32[256,256]{1,0:T(8,128)S(1)} %fusion.74), kind=kOutput, calls=%fused_computation.4.clone.1 | convolution fusion | flops 1611661312 | bytes 6553600 | tf_op jit(solution)/shard_map/while/body/eval_jaxpr/pij,pjk->pik/dot_general | solution.py:11
  235.8 4.9 %fusion.75 = f32[8,256,256]{1,2,0:T(8,128)} fusion(f32[8,256,256]{1,2,0:T(8,128)S(1)} %copy.103, f32[8,256,256]{2,1,0:T(8,128)S(1)} %fusion.73, f32[256,256]{1,0:T(8,128)S(1)} %fusion.74), kind=kOutput, calls=%fused_computation.4.clone.1 | convolution fusion | flops 1611661312 | bytes 6553600 | tf_op jit(solution)/shard_map/while/body/eval_jaxpr/pij,pjk->pik/dot_general | solution.py:11
  248.9 4.9 %fusion.75 = f32[8,256,256]{1,2,0:T(8,128)} fusion(f32[8,256,256]{1,2,0:T(8,128)S(1)} %copy.103, f32[8,256,256]{2,1,0:T(8,128)S(1)} %fusion.73, f32[256,256]{1,0:T(8,128)S(1)} %fusion.74), kind=kOutput, calls=%fused_computation.4.clone.1 | convolution fusion | flops 1611661312 | bytes 6553600 | tf_op jit(solution)/shard_map/while/body/eval_jaxpr/pij,pjk->pik/dot_general | solution.py:11
  257.4 3.7 %fusion.49 = f32[8,1,256]{2,1,0:T(1,128)S(1)} fusion(f32[8,256,1]{1,0,2:T(8,128)S(1)} %bitcast.90, f32[8,256,256]{2,1,0:T(8,128)} %get-tuple-element.24, f32[8]{0:T(128)S(1)} %sqrt.7), kind=kOutput, calls=%fused_computation.63 | convolution fusion | flops 6815744 | bytes 2113568 | tf_op jit(solution)/shard_map/pij,pj->pi/dot_general | solution.py:67
  263.1 5.9 %add_bitcast_fusion = f32[256,8,256]{0,2,1:T(8,128)} fusion(f32[256,8,256]{2,1,0:T(8,128)S(1)} %copy-done.4, f32[8,256]{1,0:T(8,128)S(1)} %bitcast.91, f32[8,256]{1,0:T(8,128)S(1)} %broadcast_multiply_fusion.1, f32[8,256,256]{2,1,0:T(8,128)S(1)} %copy-done.2, f32[8]{0:T(128)S(1)} %sqrt.7), kind=kOutput, calls=%fused_computation.28 | convolution fusion | flops 1612709888 | bytes 6307872 | tf_op jit(solution)/shard_map/pjk,jpc->kpc/dot_general | solution.py:72
  272.0 4.3 %all-to-all-start.1 = ((f32[256,8,256]{2,1,0:T(8,128)}), f32[256,8,256]{2,1,0:T(8,128)}, u32[]{:S(2)}, u32[]{:S(2)}) async-start(f32[256,8,256]{2,1,0:T(8,128)} %copy.48), calls=%async_computation.1 | async-start | bytes 4194304 | tf_op jit(solution)/shard_map/all_to_all | solution.py:73
  279.6 44.6 %all-to-all-done.1 = f32[256,8,256]{2,1,0:T(8,128)} async-done(((f32[256,8,256]{2,1,0:T(8,128)}), f32[256,8,256]{2,1,0:T(8,128)}, u32[]{:S(2)}, u32[]{:S(2)}) %all-to-all-start.1) | async-done | bytes 2097184 | tf_op jit(solution)/shard_map/all_to_all | solution.py:73
  324.2 4.1 %fusion.32 = f32[32,64,256]{2,1,0:T(8,128)} fusion(f32[32,8,8,256]{3,2,0,1:T(8,128)} %bitcast.24, s32[64]{0:T(128)S(1)} %bitcast.96), kind=kOutput, calls=%fused_computation.38 | convolution fusion | flops 402657280 | bytes 4194560 | tf_op jit(solution)/shard_map/kjc,qj->kqc/dot_general | solution.py:74
  (126 shorter events, 134.0 us)
Async XLA Ops:
  0.6 1.6 copy-start
  6.7 8.2 %copy-start.6 = (f32[1,8,512]{2,1,0:T(8,128)S(1)}, f32[1,8,512]{2,1,0:T(8,128)}, u32[]{:S(2)}) copy-start(f32[1,8,512]{2,1,0:T(8,128)} %param.15) | copy-start | bytes 49156
  6.7 8.3 %copy-start.8 = (s32[1,8]{1,0:T(1,128)S(1)}, s32[1,8]{1,0:T(1,128)}, u32[]{:S(2)}) copy-start(s32[1,8]{1,0:T(1,128)} %param.13) | copy-start | bytes 100
  6.7 55.8 %all-to-all-start = ((f32[32,64,256]{2,0,1:T(8,128)}), f32[32,64,256]{2,0,1:T(8,128)}, u32[]{:S(2)}, u32[]{:S(2)}) async-start(f32[32,64,256]{2,0,1:T(8,128)} %copy.41), calls=%async_computation | async-start | bytes 4194304 | tf_op jit(solution)/shard_map/all_to_all | solution.py:41
  71.9 3.2 copy-start.3
  71.9 3.2 copy-start.5
  81.1 4.3 %copy-start.7 = (f32[1,8,512]{2,1,0:T(8,128)S(1)}, f32[1,8,512]{2,1,0:T(8,128)}, u32[]{:S(2)}) copy-start(f32[1,8,512]{2,1,0:T(8,128)} %param.14) | copy-start | bytes 49156
  100.0 2.2 copy-start.1
  113.1 2.2 copy-start.1
  126.2 2.2 copy-start.1
  139.3 2.2 copy-start.1
  152.5 2.2 copy-start.1
  165.6 2.2 copy-start.1
  178.7 2.2 copy-start.1
  191.8 2.2 copy-start.1
  204.9 2.2 copy-start.1
  218.0 2.2 copy-start.1
  231.1 2.2 copy-start.1
  244.2 2.2 copy-start.1
  257.3 3.7 %copy-start.2 = (f32[8,256,256]{2,1,0:T(8,128)S(1)}, f32[8,256,256]{2,1,0:T(8,128)}, u32[]{:S(2)}) copy-start(f32[8,256,256]{2,1,0:T(8,128)} %get-tuple-element.24) | copy-start | bytes 6291460
  261.1 2.0 copy-start.4
  272.0 52.2 %all-to-all-start.1 = ((f32[256,8,256]{2,1,0:T(8,128)}), f32[256,8,256]{2,1,0:T(8,128)}, u32[]{:S(2)}, u32[]{:S(2)}) async-start(f32[256,8,256]{2,1,0:T(8,128)} %copy.48), calls=%async_computation.1 | async-start | bytes 4194304 | tf_op jit(solution)/shard_map/all_to_all | solution.py:73
  276.4 47.8 %copy-start.9 = (s32[1,64]{1,0:T(1,128)S(1)}, s32[1,64]{1,0:T(1,128)}, u32[]{:S(2)}) copy-start(s32[1,64]{1,0:T(1,128)} %param.11) | copy-start | bytes 772
where the time goes:
time: 329 us; the launch traced here: 328 us
  matrix products  161 us (49%)
  waiting for transfers between devices  92 us (28%)
  local copies, waits for them, and re-layouts  51.3 us (16%)
  starting transfers between devices  11.8 us (4%)
  other arithmetic  11.2 us (3%)
    dot_general x36, matrix products, batched(): jnp.einsum('pij,pjk->pik', left, right, precision=lax.Precision.HIGHEST)  128 us
    all_to_all x1, waiting for transfers between devices, local(): lax.all_to_all(listed, 'mem', split_axis=1, concat_axis=0, tiled=True)  47.5 us
    all_to_all x1, waiting for transfers between devices, local(): lax.all_to_all(updated, 'mem', split_axis=0, concat_axis=1, tiled=True)  44.6 us
    while x48, local copies, waits for them, and re-layouts  29.3 us
    all_to_all x1, starting transfers between devices, local(): lax.all_to_all(listed, 'mem', split_axis=1, concat_axis=0, tiled=True)  7.44 us
  transfers between devices with their start and end apart: 2, of which 2 were waited for; matrix products, arithmetic and copies ran while one was open for 1% of the time, Pallas kernels for 0%

commit v1 on v0

--- a/solution.py
+++ b/solution.py
@@ -38,7 +38,15 @@
     permuter = (order[None, :] == positions[:, None]).astype(jnp.float32)
     listed = jnp.einsum("kqc,qj->kjc", ensemble, permuter, precision=highest)
     my_index = lax.dynamic_slice_in_dim(obs_index[0], worker * per_worker, per_worker, 0)
-    state_in = lax.all_to_all(listed, "mem", split_axis=1, concat_axis=0, tiled=True)
+
+    def tables_balance(packet, axis_name, where_dim, array_dim=0):
+        moved = lax.axis_size(axis_name)
+        top = jnp.split(packet, moved, axis=where_dim)
+        big = jnp.stack(top, axis=0)
+        a_next = lax.all_to_all(big, axis_name, 0, 0)
+        return jnp.concatenate(a_next, array_dim)
+
+    state_in = tables_balance(listed, "mem", 1)
     obs_block = select_slots(map_columns(state_in, column_operator), my_index)
     count = obs_count[0]
     values = obs_values[0]

time: 329 us -> 327 us (level)
  other arithmetic: 11.2 us -> 7.19 us
    unnamed x19 -> x24, local copies, waits for them, and re-layouts: 4.56 us -> 9.61 us
    all_to_all x1 -> x0, local copies, waits for them, and re-layouts: 4.1 us -> none  [local(): lax.all_to_all(listed, 'mem', split_axis=1, concat_axis=0, tiled=True)]
    another operation x0 -> x2, local copies, waits for them, and re-layouts: none -> 3.36 us  [the longest x1 2.64 us: map_columns(): flat_rows = states.reshape(rows * patches * (cells // levels), levels)]
where the time goes in v1:
time: 327 us; the launch traced here: 326 us
  matrix products  161 us (49%)
  waiting for transfers between devices  92 us (28%)
  local copies, waits for them, and re-layouts  53.3 us (16%)
  starting transfers between devices  11.8 us (4%)
  other arithmetic  7.19 us (2%)
    dot_general x36, matrix products, batched(): jnp.einsum('pij,pjk->pik', left, right, precision=lax.Precision.HIGHEST)  128 us
    all_to_all x1, waiting for transfers between devices, tables_balance(): a_next = lax.all_to_all(big, axis_name, 0, 0)  47.5 us
    all_to_all x1, waiting for transfers between devices, local(): lax.all_to_all(updated, 'mem', split_axis=0, concat_axis=1, tiled=True)  44.6 us
    while x48, local copies, waits for them, and re-layouts  29.3 us
    unnamed x24, local copies, waits for them, and re-layouts  9.61 us
    all_to_all x1, starting transfers between devices, tables_balance(): a_next = lax.all_to_all(big, axis_name, 0, 0)  7.44 us
  transfers between devices with their start and end apart: 2, of which 2 were waited for; matrix products, arithmetic and copies ran while one was open for 1% of the time, Pallas kernels for 0%

profile of v1, /device:TPU:0, one launch (start us, length us, event | category | flops | bytes accessed | tf_op | source)
XLA Modules:
  0.0 326.1 jit_solution(5703119997916158694)
XLA Ops:
  9.9 7.4 %all-to-all-start = ((f32[8,32,8,256]{3,2,1,0:T(8,128)}), f32[8,32,8,256]{3,2,1,0:T(8,128)}, u32[]{:S(2)}, u32[]{:S(2)}) async-start(f32[8,32,8,256]{3,2,1,0:T(8,128)} %fusion.38), calls=%async_computation | async-start | bytes 4194304 | tf_op jit(solution)/shard_map/all_to_all | solution.py:46
  18.2 47.5 %all-to-all-done = f32[8,32,8,256]{3,2,1,0:T(8,128)} async-done(((f32[8,32,8,256]{3,2,1,0:T(8,128)}), f32[8,32,8,256]{3,2,1,0:T(8,128)}, u32[]{:S(2)}, u32[]{:S(2)}) %all-to-all-start) | async-done | bytes 2097184 | tf_op jit(solution)/shard_map/all_to_all | solution.py:46
  73.1 4.7 %fusion.62 = f32[4096,128]{1,0:T(8,128)} fusion(f32[4096,128]{1,0:T(8,128)} %reshape_reshape.3, f32[128,128]{1,0:T(8,128)S(1)} %copy-done.4), kind=kOutput, calls=%fused_computation.85 | convolution fusion | flops 805306368 | bytes 4259840 | tf_op jit(solution)/shard_map/dot_general | solution.py:18
  80.7 4.3 %bitcast_reduce_fusion = (f32[8,512]{1,0:T(8,128)S(1)}, f32[8,512,256]{1,2,0:T(8,128)S(1)}) fusion(f32[256,8,256]{2,1,0:T(8,128)} %reshape.71, s32[8,512]{1,0:T(8,128)S(1)} %dynamic-slice_bitcast_fusion), kind=kOutput, calls=%fused_computation.16 | convolution fusion | flops 3223318528 | bytes 6324224 | tf_op jit(solution)/shard_map/kpc,pco->kpo/dot_general | solution.py:26
  85.1 3.7 %fusion.15 = f32[8,1,256]{2,1,0:T(1,128)S(1)} fusion(f32[8,512,256]{1,2,0:T(8,128)S(1)} %get-tuple-element.51, f32[8,512]{1,0:T(8,128)S(1)} %get-tuple-element.49, f32[8,512,1]{1,0,2:T(8,128)S(1)} %get-tuple-element.48), kind=kOutput, calls=%fused_computation.19 | convolution fusion | flops 13631488 | bytes 4235264 | tf_op jit(solution)/shard_map/kpo,po->pk/dot_general | solution.py:74
  88.8 4.7 %select_reduce_fusion = (f32[8]{0:T(128)S(1)}, f32[8,256,256]{2,1,0:T(8,128)S(1)}) fusion(f32[256,256]{1,0:T(8,128)S(1)} %fusion.47, pred[256,256]{1,0:T(8,128)(4,1)S(1)} %iota_compare_fusion.3, f32[8,512,256]{1,2,0:T(8,128)S(1)} %get-tuple-element.51, f32[8,512]{1,0:T(8,128)S(1)} %get-tuple-element.49, f32[8,512]{1,0:T(8,128)S(1)} %select_bitcast_fusion), kind=kOutput, calls=%fused_computation.27 | convolution fusion | flops 3225944064 | bytes 6651936 | tf_op jit(solution)/shard_map/kpo,jpo->pkj/dot_general | solution.py:60
  99.6 157.3 %while.13 = (s32[]{:T(128)}, f32[8,256,256]{1,2,0:T(8,128)}, f32[8,256,256]{2,1,0:T(8,128)}, s32[]{:T(128)}) while((s32[]{:T(128)}, f32[8,256,256]{1,2,0:T(8,128)}, f32[8,256,256]{2,1,0:T(8,128)}, s32[]{:T(128)}) %tuple.31), condition=%wide.region_4.5_spmd.clone, body=%wide.region_3.4_spmd.clone.sunk | while | flops 4834066432 | bytes 36438096 | solution.py:71
  107.8 4.9 %fusion.84 = f32[8,256,256]{1,2,0:T(8,128)} fusion(f32[8,256,256]{1,2,0:T(8,128)S(1)} %copy.88, f32[8,256,256]{2,1,0:T(8,128)S(1)} %fusion.82, f32[256,256]{1,0:T(8,128)S(1)} %fusion.83), kind=kOutput, calls=%fused_computation.4.clone.1 | convolution fusion | flops 1611661312 | bytes 6553600 | tf_op jit(solution)/shard_map/while/body/eval_jaxpr/pij,pjk->pik/dot_general | solution.py:11
  120.9 4.9 %fusion.84 = f32[8,256,256]{1,2,0:T(8,128)} fusion(f32[8,256,256]{1,2,0:T(8,128)S(1)} %copy.88, f32[8,256,256]{2,1,0:T(8,128)S(1)} %fusion.82, f32[256,256]{1,0:T(8,128)S(1)} %fusion.83), kind=kOutput, calls=%fused_computation.4.clone.1 | convolution fusion | flops 1611661312 | bytes 6553600 | tf_op jit(solution)/shard_map/while/body/eval_jaxpr/pij,pjk->pik/dot_general | solution.py:11
  134.0 4.9 %fusion.84 = f32[8,256,256]{1,2,0:T(8,128)} fusion(f32[8,256,256]{1,2,0:T(8,128)S(1)} %copy.88, f32[8,256,256]{2,1,0:T(8,128)S(1)} %fusion.82, f32[256,256]{1,0:T(8,128)S(1)} %fusion.83), kind=kOutput, calls=%fused_computation.4.clone.1 | convolution fusion | flops 1611661312 | bytes 6553600 | tf_op jit(solution)/shard_map/while/body/eval_jaxpr/pij,pjk->pik/dot_general | solution.py:11
  147.1 4.9 %fusion.84 = f32[8,256,256]{1,2,0:T(8,128)} fusion(f32[8,256,256]{1,2,0:T(8,128)S(1)} %copy.88, f32[8,256,256]{2,1,0:T(8,128)S(1)} %fusion.82, f32[256,256]{1,0:T(8,128)S(1)} %fusion.83), kind=kOutput, calls=%fused_computation.4.clone.1 | convolution fusion | flops 1611661312 | bytes 6553600 | tf_op jit(solution)/shard_map/while/body/eval_jaxpr/pij,pjk->pik/dot_general | solution.py:11
  160.2 4.9 %fusion.84 = f32[8,256,256]{1,2,0:T(8,128)} fusion(f32[8,256,256]{1,2,0:T(8,128)S(1)} %copy.88, f32[8,256,256]{2,1,0:T(8,128)S(1)} %fusion.82, f32[256,256]{1,0:T(8,128)S(1)} %fusion.83), kind=kOutput, calls=%fused_computation.4.clone.1 | convolution fusion | flops 1611661312 | bytes 6553600 | tf_op jit(solution)/shard_map/while/body/eval_jaxpr/pij,pjk->pik/dot_general | solution.py:11
  173.4 4.9 %fusion.84 = f32[8,256,256]{1,2,0:T(8,128)} fusion(f32[8,256,256]{1,2,0:T(8,128)S(1)} %copy.88, f32[8,256,256]{2,1,0:T(8,128)S(1)} %fusion.82, f32[256,256]{1,0:T(8,128)S(1)} %fusion.83), kind=kOutput, calls=%fused_computation.4.clone.1 | convolution fusion | flops 1611661312 | bytes 6553600 | tf_op jit(solution)/shard_map/while/body/eval_jaxpr/pij,pjk->pik/dot_general | solution.py:11
  186.5 4.9 %fusion.84 = f32[8,256,256]{1,2,0:T(8,128)} fusion(f32[8,256,256]{1,2,0:T(8,128)S(1)} %copy.88, f32[8,256,256]{2,1,0:T(8,128)S(1)} %fusion.82, f32[256,256]{1,0:T(8,128)S(1)} %fusion.83), kind=kOutput, calls=%fused_computation.4.clone.1 | convolution fusion | flops 1611661312 | bytes 6553600 | tf_op jit(solution)/shard_map/while/body/eval_jaxpr/pij,pjk->pik/dot_general | solution.py:11
  199.6 4.9 %fusion.84 = f32[8,256,256]{1,2,0:T(8,128)} fusion(f32[8,256,256]{1,2,0:T(8,128)S(1)} %copy.88, f32[8,256,256]{2,1,0:T(8,128)S(1)} %fusion.82, f32[256,256]{1,0:T(8,128)S(1)} %fusion.83), kind=kOutput, calls=%fused_computation.4.clone.1 | convolution fusion | flops 1611661312 | bytes 6553600 | tf_op jit(solution)/shard_map/while/body/eval_jaxpr/pij,pjk->pik/dot_general | solution.py:11
  212.7 4.9 %fusion.84 = f32[8,256,256]{1,2,0:T(8,128)} fusion(f32[8,256,256]{1,2,0:T(8,128)S(1)} %copy.88, f32[8,256,256]{2,1,0:T(8,128)S(1)} %fusion.82, f32[256,256]{1,0:T(8,128)S(1)} %fusion.83), kind=kOutput, calls=%fused_computation.4.clone.1 | convolution fusion | flops 1611661312 | bytes 6553600 | tf_op jit(solution)/shard_map/while/body/eval_jaxpr/pij,pjk->pik/dot_general | solution.py:11
  225.8 4.9 %fusion.84 = f32[8,256,256]{1,2,0:T(8,128)} fusion(f32[8,256,256]{1,2,0:T(8,128)S(1)} %copy.88, f32[8,256,256]{2,1,0:T(8,128)S(1)} %fusion.82, f32[256,256]{1,0:T(8,128)S(1)} %fusion.83), kind=kOutput, calls=%fused_computation.4.clone.1 | convolution fusion | flops 1611661312 | bytes 6553600 | tf_op jit(solution)/shard_map/while/body/eval_jaxpr/pij,pjk->pik/dot_general | solution.py:11
  238.9 4.9 %fusion.84 = f32[8,256,256]{1,2,0:T(8,128)} fusion(f32[8,256,256]{1,2,0:T(8,128)S(1)} %copy.88, f32[8,256,256]{2,1,0:T(8,128)S(1)} %fusion.82, f32[256,256]{1,0:T(8,128)S(1)} %fusion.83), kind=kOutput, calls=%fused_computation.4.clone.1 | convolution fusion | flops 1611661312 | bytes 6553600 | tf_op jit(solution)/shard_map/while/body/eval_jaxpr/pij,pjk->pik/dot_general | solution.py:11
  252.0 4.9 %fusion.84 = f32[8,256,256]{1,2,0:T(8,128)} fusion(f32[8,256,256]{1,2,0:T(8,128)S(1)} %copy.88, f32[8,256,256]{2,1,0:T(8,128)S(1)} %fusion.82, f32[256,256]{1,0:T(8,128)S(1)} %fusion.83), kind=kOutput, calls=%fused_computation.4.clone.1 | convolution fusion | flops 1611661312 | bytes 6553600 | tf_op jit(solution)/shard_map/while/body/eval_jaxpr/pij,pjk->pik/dot_general | solution.py:11
  256.9 3.7 %fusion.58 = f32[8,1,256]{2,1,0:T(1,128)S(1)} fusion(f32[8,256,1]{1,0,2:T(8,128)S(1)} %bitcast.115, f32[8,256,256]{2,1,0:T(8,128)} %get-tuple-element.24, f32[8]{0:T(128)S(1)} %sqrt.7), kind=kOutput, calls=%fused_computation.78 | convolution fusion | flops 6815744 | bytes 2113568 | tf_op jit(solution)/shard_map/pij,pj->pi/dot_general | solution.py:75
  262.7 4.0 %add_bitcast_fusion = f32[256,8,256]{0,2,1:T(8,128)} fusion(f32[256,8,256]{0,2,1:T(8,128)S(1)} %copy-done.3, f32[8,256]{1,0:T(8,128)S(1)} %bitcast.116, f32[8,256]{1,0:T(8,128)S(1)} %broadcast_multiply_fusion.1, f32[8,256,256]{2,1,0:T(8,128)S(1)} %copy-done.2, f32[8]{0:T(128)S(1)} %sqrt.7), kind=kOutput, calls=%fused_computation.24 | convolution fusion | flops 1613234176 | bytes 6307872 | tf_op jit(solution)/shard_map/pjk,jpc->kpc/dot_general | solution.py:80
  269.7 4.3 %all-to-all-start.1 = ((f32[256,8,256]{2,1,0:T(8,128)}), f32[256,8,256]{2,1,0:T(8,128)}, u32[]{:S(2)}, u32[]{:S(2)}) async-start(f32[256,8,256]{2,1,0:T(8,128)} %copy.33), calls=%async_computation.1 | async-start | bytes 4194304 | tf_op jit(solution)/shard_map/all_to_all | solution.py:81
  277.3 44.6 %all-to-all-done.1 = f32[256,8,256]{2,1,0:T(8,128)} async-done(((f32[256,8,256]{2,1,0:T(8,128)}), f32[256,8,256]{2,1,0:T(8,128)}, u32[]{:S(2)}, u32[]{:S(2)}) %all-to-all-start.1) | async-done | bytes 2097184 | tf_op jit(solution)/shard_map/all_to_all | solution.py:81
  321.9 4.1 %fusion.32 = f32[32,64,256]{2,1,0:T(8,128)} fusion(f32[32,8,8,256]{3,2,0,1:T(8,128)} %bitcast.27, s32[64]{0:T(128)S(1)} %bitcast.121), kind=kOutput, calls=%fused_computation.36 | convolution fusion | flops 402657280 | bytes 4194560 | tf_op jit(solution)/shard_map/kjc,qj->kqc/dot_general | solution.py:82
  (130 shorter events, 132.9 us)
Async XLA Ops:
  0.6 1.6 copy-start
  9.9 8.2 %copy-start.5 = (f32[1,8,512]{2,1,0:T(8,128)S(1)}, f32[1,8,512]{2,1,0:T(8,128)}, u32[]{:S(2)}) copy-start(f32[1,8,512]{2,1,0:T(8,128)} %param.15) | copy-start | bytes 49156
  9.9 8.3 %copy-start.7 = (s32[1,8]{1,0:T(1,128)S(1)}, s32[1,8]{1,0:T(1,128)}, u32[]{:S(2)}) copy-start(s32[1,8]{1,0:T(1,128)} %param.13) | copy-start | bytes 100
  9.9 55.8 %all-to-all-start = ((f32[8,32,8,256]{3,2,1,0:T(8,128)}), f32[8,32,8,256]{3,2,1,0:T(8,128)}, u32[]{:S(2)}, u32[]{:S(2)}) async-start(f32[8,32,8,256]{3,2,1,0:T(8,128)} %fusion.38), calls=%async_computation | async-start | bytes 4194304 | tf_op jit(solution)/shard_map/all_to_all | solution.py:46
  70.4 2.6 copy-start.4
  80.7 4.3 %copy-start.6 = (f32[1,8,512]{2,1,0:T(8,128)S(1)}, f32[1,8,512]{2,1,0:T(8,128)}, u32[]{:S(2)}) copy-start(f32[1,8,512]{2,1,0:T(8,128)} %param.14) | copy-start | bytes 49156
  99.6 2.2 copy-start.1
  112.7 2.2 copy-start.1
  125.8 2.2 copy-start.1
  138.9 2.2 copy-start.1
  152.0 2.2 copy-start.1
  165.2 2.2 copy-start.1
  178.3 2.2 copy-start.1
  191.4 2.2 copy-start.1
  204.5 2.2 copy-start.1
  217.6 2.2 copy-start.1
  230.7 2.2 copy-start.1
  243.8 2.2 copy-start.1
  256.9 3.7 %copy-start.2 = (f32[8,256,256]{2,1,0:T(8,128)S(1)}, f32[8,256,256]{2,1,0:T(8,128)}, u32[]{:S(2)}) copy-start(f32[8,256,256]{2,1,0:T(8,128)} %get-tuple-element.24) | copy-start | bytes 6291460
  260.7 2.0 copy-start.3
  269.7 52.2 %all-to-all-start.1 = ((f32[256,8,256]{2,1,0:T(8,128)}), f32[256,8,256]{2,1,0:T(8,128)}, u32[]{:S(2)}, u32[]{:S(2)}) async-start(f32[256,8,256]{2,1,0:T(8,128)} %copy.33), calls=%async_computation.1 | async-start | bytes 4194304 | tf_op jit(solution)/shard_map/all_to_all | solution.py:81
  274.1 47.8 %copy-start.8 = (s32[1,64]{1,0:T(1,128)S(1)}, s32[1,64]{1,0:T(1,128)}, u32[]{:S(2)}) copy-start(s32[1,64]{1,0:T(1,128)} %param.11) | copy-start | bytes 772
